TPU v7x, 256 devices: a whole 4x4x8 slice. The times are simulated.
256 devices in a mesh: cuts: 64 (over x, y, z_lo), frame: 4 (over z_hi, core).
Axes of the slice: x: 4, y: 4, z: 8 (z_hi: 2, z_lo: 4; z = z_hi * 4 + z_lo), core: 2. Of those that a mesh axis runs over, the one named last changes fastest.
Arguments:
- basis: bfloat16 [2, 32, 128, 4, 256], P(None, None, 'cuts', 'frame'), may hold values from -6 to 6
- coil_maps: bfloat16 [2, 12, 128, 4, 256], P(None, None, 'cuts', 'frame'), may hold values from -3 to 3
- factors: bfloat16 [2, 32, 64], P(None, None, 'frame'), may hold values from -0.75 to 0.75
- lines: int32 [64, 128], P(None, 'cuts'), may hold values from 0 to 511
- kdata: bfloat16 [2, 64, 128, 12, 4], P(None, None, 'cuts', None, 'frame'), may hold values from -6 to 6
Outputs:
- basis_grad: float32 [2, 32, 128, 4, 256], P(None, None, 'cuts', 'frame')
- factor_grad: float32 [2, 32, 64], P(None, None, 'frame')
Inputs may be any that keep to these rules, and one draw needn't show every extreme that they name: lines[t, j] = (ky - (j // 2) * 4) * 128 + kz for a position (ky, kz) sampled in frame t whose ky lies in the rows (j // 2) * 4 to (j // 2 + 1) * 4 - 1; positions may repeat over frames.
All inputs are finite; a program needn't handle non-finite values.
Results may differ from a plain program's by a relative error of at most 0.011.
Values may be sent and summed in bfloat16 or wider, within the bound.
A program may use at most 64 MiB of HBM per device.

v0:
```python
import math
import jax
import jax.numpy as jnp
import numpy as np
from jax import lax
from jax.sharding import PartitionSpec as P

BF = jnp.bfloat16
F32 = jnp.float32


def dft_np(size):
    index = np.arange(size)
    angle = index[:, None] * index[None, :] % size * (2.0 * math.pi / size)
    return (np.cos(angle) / math.sqrt(size), -np.sin(angle) / math.sqrt(size))


def dot(spec, a, b):
    return jnp.einsum(spec, a, b, preferred_element_type=F32)


def body(basis, coil_maps, factors, lines, kdata):
    n_cuts = lax.axis_size("cuts")
    cuts = lax.axis_index("cuts")
    rank, slab, width = (basis.shape[1], basis.shape[2], basis.shape[4])
    coils = coil_maps.shape[1]
    depth = slab * n_cuts
    rows = width // n_cuts
    lpd = lines.shape[1]
    scale = 1.0 / math.sqrt(coils * lpd * n_cuts * basis.shape[3] * lax.axis_size("frame"))
    cy, sy = dft_np(width)
    perm = (np.arange(rows)[:, None] + rows * np.arange(n_cuts)[None, :]).reshape(-1)
    c, s = (cy[:, perm], sy[:, perm])
    table = jnp.asarray(np.block([[c, s], [-s, c]]), BF)
    v = lax.all_gather(factors, "frame", axis=2, tiled=True)
    frames = v.shape[2]
    every = lax.all_gather(lines, "cuts", axis=0)
    kz = every % depth
    row = every // depth
    b = basis[:, :, :, 0].astype(F32)
    m = coil_maps[:, :, :, 0].astype(F32)
    image = jnp.stack(
        [
            m[0][:, :, None] * b[0].transpose(1, 0, 2)[None]
            - m[1][:, :, None] * b[1].transpose(1, 0, 2)[None],
            m[0][:, :, None] * b[1].transpose(1, 0, 2)[None]
            + m[1][:, :, None] * b[0].transpose(1, 0, 2)[None],
        ],
        axis=3,
    ).astype(BF)
    image = image.reshape(coils * slab * rank, 2 * width)
    hybrid = jnp.dot(image, table, preferred_element_type=F32).astype(BF)
    hybrid = hybrid.reshape(coils, slab, rank, 2, width)
    vr, vi = (v[0], v[1])
    mixer = jnp.stack([jnp.stack([vr, -vi]), jnp.stack([vi, vr])])
    mixed = dot("czlpw,qplt->czqtw", hybrid, mixer).reshape(coils, slab, 2, frames, rows, n_cuts)
    zpos = cuts * slab + jnp.arange(slab)
    angle = (kz[None] * zpos[:, None, None, None] % depth).astype(F32) * (2.0 * math.pi / depth)
    pr = (jnp.cos(angle) / math.sqrt(depth)).astype(BF).astype(F32)
    pi = (-jnp.sin(angle) / math.sqrt(depth)).astype(BF).astype(F32)
    pr = pr.transpose(0, 3, 2, 1)
    pi = pi.transpose(0, 3, 2, 1)
    row = row.transpose(2, 1, 0)
    parts = []
    for sample in range(lpd):
        r = row[sample]
        sel = sum((jnp.where(r == k, mixed[:, :, :, :, k], 0.0) for k in range(rows)))
        re = jnp.sum(sel[:, :, 0] * pr[None, :, sample] - sel[:, :, 1] * pi[None, :, sample], 1)
        im = jnp.sum(sel[:, :, 0] * pi[None, :, sample] + sel[:, :, 1] * pr[None, :, sample], 1)
        parts.append(jnp.stack([re, im]))
    part = jnp.stack(parts)
    part = part.transpose(4, 2, 1, 0, 3).reshape(n_cuts, -1).astype(BF)
    pred = lax.psum_scatter(part, "cuts", scatter_dimension=0, tiled=True)
    kd = kdata[..., 0].transpose(3, 0, 2, 1).reshape(1, -1)
    resid = (pred.astype(F32) - kd.astype(F32)).astype(BF)
    whole = lax.all_gather(resid, "cuts", axis=0, tiled=True)
    whole = whole.reshape(n_cuts, coils, 2, lpd, frames).transpose(3, 2, 1, 4, 0).astype(F32)
    spread = 0.0
    for sample in range(lpd):
        x, y = (whole[sample, 0][:, None], whole[sample, 1][:, None])
        re = x * pr[None, :, sample] + y * pi[None, :, sample]
        im = y * pr[None, :, sample] - x * pi[None, :, sample]
        e = jnp.stack([re, im], 2)
        r = row[sample]
        spread = spread + jnp.stack([jnp.where(r == k, e, 0.0) for k in range(rows)], 4)
    spread = spread.astype(BF).reshape(coils, slab, 2, frames, width)
    outer = dot("czlpw,czqtw->plqt", hybrid, spread)
    gv = jnp.stack([outer[0, :, 0] + outer[1, :, 1], outer[0, :, 1] - outer[1, :, 0]])
    unmix = jnp.stack([jnp.stack([vr, vi]), jnp.stack([-vi, vr])])
    zgrad = dot("czptw,qplt->czlqw", spread, unmix).astype(BF)
    zgrad = zgrad.reshape(coils * slab * rank, 2 * width)
    back = lax.dot_general(zgrad, table, (((1,), (1,)), ((), ())), preferred_element_type=F32)
    back = back.reshape(coils, slab, rank, 2, width)
    gr = jnp.sum(m[0][:, :, None] * back[:, :, :, 0] + m[1][:, :, None] * back[:, :, :, 1], 0)
    gi = jnp.sum(m[0][:, :, None] * back[:, :, :, 1] - m[1][:, :, None] * back[:, :, :, 0], 0)
    grad = jnp.stack([gr, gi]).transpose(0, 2, 1, 3)[:, :, :, None]
    shared = lax.psum_scatter(gv * scale, "frame", scatter_dimension=2, tiled=True)
    return (grad, lax.psum(shared, "cuts"))


def solution(mesh):
    placed = (
        P(None, None, "cuts", "frame", None),
        P(None, None, "cuts", "frame", None),
        P(None, None, "frame"),
        P(None, "cuts"),
        P(None, None, "cuts", None, "frame"),
    )
    return jax.shard_map(
        body,
        mesh=mesh,
        in_specs=placed,
        out_specs=(P(None, None, "cuts", "frame", None), P(None, None, "frame")),
        check_vma=False,
    )
```

profile of v0, /device:TPU:0, one launch (start us, length us, event | category | flops | bytes accessed | tf_op | source)
XLA Modules:
  0.0 1550.7 jit_solution(7144732709453119394)
XLA Ops:
  7.2 0.0 all-reduce.4.cloned.1.call-start
  7.2 0.7 copy.101
  7.9 9.1 all_gather.12
  17.0 0.1 copy.102
  17.1 0.8 convert_element_type.92
  17.9 186.8 %all-gather.1 = s32[64,64,2]{1,2,0:T(2,128)S(1)} all-gather(s32[1,64,2]{1,2,0:T(2,128)} %bitcast.244), channel_id=2, replica_groups=mesh['cuts'=64,'frame'=4] {'cuts'}, dimensions={0}, use_global_device_ids=true | all-gather | bytes 33280 | tf_op jit(solution)/shard_map/all_gather | solution.py:37
  204.8 0.1 copy.105
  204.8 0.1 fusion.24
  205.0 0.9 convert_element_type.93
  206.0 0.6 fusion.25
  206.7 1.6 subtract_convert_fusion
  208.3 0.0 copy-start.32
  208.3 1.8 pad_maximum_fusion.2
  210.1 0.2 copy.146
  210.3 0.6 convolution_convert_fusion
  210.9 1.1 reshape.326
  212.0 0.6 fusion.33
  212.6 1.7 convolution_bitcast_fusion
  214.3 4.4 reshape.327
  218.7 12.0 fusion.43
  230.8 0.8 select_add_fusion.1
  231.6 0.3 subtract_reduce_fusion.2
  231.9 0.1 maximum_bitcast_fusion.1
  232.0 0.3 subtract_reduce_fusion.1
  232.3 0.1 maximum_bitcast_fusion.2
  232.4 0.2 maximum_bitcast_fusion
  232.6 0.8 copy.115
  233.4 1.3 convert_element_type.102
  234.7 0.0 all-reduce.4.cloned.1.call-update
  234.8 0.7 dynamic-slice.2
  235.4 0.6 dynamic-slice
  236.0 0.1 reshape.328
  236.8 682.6 %all-reduce.4.cloned.1.call-done = bf16[64,3072]{1,0:T(8,128)(2,1)} async-done(((bf16[64,3072]{1,0:T(8,128)(2,1)}), bf16[64,3072]{1,0:T(8,128)(2,1)}) %all-reduce.4.cloned.1.call-update) | async-done | bytes 393232
  919.5 1.4 fusion.40
  920.8 188.8 %all-gather.2 = bf16[64,1,3072]{2,1,0:T(2,128)(2,1)S(1)} all-gather(bf16[1,1,3072]{2,1,0:T(2,128)(2,1)S(1)} %fusion.40), channel_id=1, replica_groups=mesh['cuts'=64,'frame'=4] {'cuts'}, dimensions={0}, use_global_device_ids=true | all-gather | bytes 399360 | tf_op jit(solution)/shard_map/all_gather | solution.py:76
  1109.6 2.2 convert_reduce_fusion
  1111.8 1.1 reshape.329
  1113.0 1.2 fusion.44
  1114.2 0.3 copy.120
  1114.5 0.3 copy.121
  1114.8 0.3 copy.118
  1115.2 0.3 copy.117
  1115.5 0.2 multiply_add_fusion.1
  1115.8 0.2 copy-done.2
  1116.0 0.0 copy-done.4
  1116.0 0.2 multiply_add_fusion
  1116.3 0.2 copy-done.29
  1116.5 3.5 broadcast_select_fusion.3
  1120.1 3.6 broadcast_select_fusion.7
  1123.7 12.3 broadcast_select_fusion.2
  1136.0 14.7 fusion
  1150.7 3.0 reshape.347
  1153.7 3.0 convert_element_type.113
  1156.6 2.6 fusion.11
  1159.3 0.4 fusion.8
  1159.7 0.8 copy.124
  1160.5 0.5 reshape.345
  1161.0 0.1 copy.129
  1161.1 18.8 %all-reduce.1 = f32[2,32,64]{1,0,2:T(2,128)S(1)} all-reduce(f32[2,32,64]{1,0,2:T(2,128)S(1)} %copy.129), channel_id=4, replica_groups=mesh['cuts'=64,'frame'=4] {'frame'}, use_global_device_ids=true, to_apply=%region_7.8.clone | all-reduce | flops 4096 | bytes 32768
  1180.0 361.6 %psum.7 = f32[2,32,16]{1,0,2:T(2,128)S(1)} all-reduce(f32[2,32,16]{1,0,2:T(2,128)S(1)} %constant_dynamic-slice_fusion), channel_id=1, replica_groups=mesh['cuts'=64,'frame'=4] {'cuts'}, use_global_device_ids=true, to_apply=%region_8.9 | all-reduce | flops 1024 | bytes 8192 | tf_op jit(solution)/shard_map/psum | solution.py:98
  1541.6 0.6 copy.131
  1542.2 0.6 fusion.15
  1542.8 0.2 add_reduce_fusion
  1543.1 0.8 copy.130
  (82 shorter events, 0.3 us)
Async XLA Ops:
  7.2 912.3 %all-reduce.4.cloned.1.call-start = ((), (), s32[]{:S(2)}) async-start(), calls=%async_computation | async-start | bytes 786432
  17.9 190.4 %copy-start.10 = (f32[12,2,256]{2,1,0:T(2,128)}, f32[12,2,256]{2,1,0:T(2,128)S(1)}, u32[]{:S(2)}) copy-start(f32[12,2,256]{2,1,0:T(2,128)S(1)} %get-tuple-element.60) | copy-start | bytes 73732
  17.9 190.4 %copy-start.12 = (f32[12,2,256]{2,1,0:T(2,128)}, f32[12,2,256]{2,1,0:T(2,128)S(1)}, u32[]{:S(2)}) copy-start(f32[12,2,256]{2,1,0:T(2,128)S(1)} %get-tuple-element.61) | copy-start | bytes 73732
  205.0 25.8 %copy-start.14 = (pred[64,64]{1,0:T(8,128)(4,1)}, pred[64,64]{1,0:T(8,128)(4,1)S(1)}, u32[]{:S(2)}) copy-start(pred[64,64]{1,0:T(8,128)(4,1)S(1)} %get-tuple-element.50) | copy-start | bytes 12292
  205.0 25.8 %copy-start.16 = (pred[64,64]{1,0:T(8,128)(4,1)}, pred[64,64]{1,0:T(8,128)(4,1)S(1)}, u32[]{:S(2)}) copy-start(pred[64,64]{1,0:T(8,128)(4,1)S(1)} %get-tuple-element.51) | copy-start | bytes 12292
  205.0 25.8 %copy-start.18 = (pred[64,64]{1,0:T(8,128)(4,1)}, pred[64,64]{1,0:T(8,128)(4,1)S(1)}, u32[]{:S(2)}) copy-start(pred[64,64]{1,0:T(8,128)(4,1)S(1)} %get-tuple-element.52) | copy-start | bytes 12292
  205.0 25.8 %copy-start.20 = (pred[64,64]{1,0:T(8,128)(4,1)}, pred[64,64]{1,0:T(8,128)(4,1)S(1)}, u32[]{:S(2)}) copy-start(pred[64,64]{1,0:T(8,128)(4,1)S(1)} %get-tuple-element.53) | copy-start | bytes 12292
  205.0 25.8 %copy-start.22 = (pred[64,64]{1,0:T(8,128)(4,1)}, pred[64,64]{1,0:T(8,128)(4,1)S(1)}, u32[]{:S(2)}) copy-start(pred[64,64]{1,0:T(8,128)(4,1)S(1)} %get-tuple-element.54) | copy-start | bytes 12292
  205.0 25.8 %copy-start.24 = (pred[64,64]{1,0:T(8,128)(4,1)}, pred[64,64]{1,0:T(8,128)(4,1)S(1)}, u32[]{:S(2)}) copy-start(pred[64,64]{1,0:T(8,128)(4,1)S(1)} %get-tuple-element.55) | copy-start | bytes 12292
  205.0 25.8 %copy-start.26 = (pred[64,64]{1,0:T(8,128)(4,1)}, pred[64,64]{1,0:T(8,128)(4,1)S(1)}, u32[]{:S(2)}) copy-start(pred[64,64]{1,0:T(8,128)(4,1)S(1)} %get-tuple-element.57) | copy-start | bytes 12292
  205.0 25.8 %copy-start.28 = (pred[64,64]{1,0:T(8,128)(4,1)}, pred[64,64]{1,0:T(8,128)(4,1)S(1)}, u32[]{:S(2)}) copy-start(pred[64,64]{1,0:T(8,128)(4,1)S(1)} %get-tuple-element.56) | copy-start | bytes 12292
  206.6 25.0 %copy-start.5 = (f32[2,64,64]{2,1,0:T(8,128)}, f32[2,64,64]{2,1,0:T(8,128)S(1)}, u32[]{:S(2)}) copy-start(f32[2,64,64]{2,1,0:T(8,128)S(1)} %get-tuple-element.42) | copy-start | bytes 98308
  206.6 25.4 %copy-start.1 = (f32[2,64,64]{2,1,0:T(8,128)}, f32[2,64,64]{2,1,0:T(8,128)S(1)}, u32[]{:S(2)}) copy-start(f32[2,64,64]{2,1,0:T(8,128)S(1)} %get-tuple-element.43) | copy-start | bytes 98308
  206.6 25.0 %copy-start.7 = (f32[2,64,64]{2,1,0:T(8,128)}, f32[2,64,64]{2,1,0:T(8,128)S(1)}, u32[]{:S(2)}) copy-start(f32[2,64,64]{2,1,0:T(8,128)S(1)} %get-tuple-element.45) | copy-start | bytes 98308
  206.7 25.4 %copy-start.3 = (f32[2,64,64]{2,1,0:T(8,128)}, f32[2,64,64]{2,1,0:T(8,128)S(1)}, u32[]{:S(2)}) copy-start(f32[2,64,64]{2,1,0:T(8,128)S(1)} %get-tuple-element.44) | copy-start | bytes 98308
  208.3 2.0 copy-start.32
  232.6 2.2 copy-start.34
  232.6 2.8 copy-start.33
  232.6 3.4 copy-start.31
  1114.2 1.3 copy-start.6
  1114.2 1.3 copy-start.8
  1115.2 0.8 copy-start.2
  1115.2 0.9 copy-start.4
  1115.8 0.7 copy-start.29
  1116.5 3.5 copy-start.27
  1120.0 3.6 copy-start.15
  1120.0 3.6 copy-start.17
  1120.0 3.6 copy-start.19
  1120.1 3.6 copy-start.21
  1120.1 3.6 copy-start.23
  1120.1 3.6 copy-start.25
  1156.6 2.6 copy-start
  1156.6 2.6 copy-start.30
  1159.7 382.5 %copy-start.9 = (bf16[2,256,512,1,1]{2,1,0,4,3:T(8,128)(2,1)S(1)}, bf16[2,256,512,1,1]{2,1,0,4,3:T(8,128)(2,1)}, u32[]{:S(2)}) copy-start(bf16[2,256,512,1,1]{2,1,0,4,3:T(8,128)(2,1)} %constant.75) | copy-start | bytes 1572868
  1161.1 381.7 %copy-start.11 = (f32[12,2,256]{2,1,0:T(2,128)S(1)}, f32[12,2,256]{2,1,0:T(2,128)}, u32[]{:S(2)}) copy-start(f32[12,2,256]{2,1,0:T(2,128)} %copy-done.10) | copy-start | bytes 73732
  1161.1 381.7 %copy-start.13 = (f32[12,2,256]{2,1,0:T(2,128)S(1)}, f32[12,2,256]{2,1,0:T(2,128)}, u32[]{:S(2)}) copy-start(f32[12,2,256]{2,1,0:T(2,128)} %copy-done.12) | copy-start | bytes 73732
Sparse Core Ops, SparseCore 0:
  234.9 684.5 all-reduce.3
where the time goes:
time: 1550 us
  blocking collectives  765 us (49%)
  waiting for transfers between devices  683 us (44%)
  other arithmetic  46.4 us (3%)
  local copies, waits for them, and re-layouts  35 us (2%)
  between operations  15.6 us (1%)
    unnamed x2, waiting for transfers between devices  683 us
    psum x1, blocking collectives, body(): return (grad, lax.psum(shared, 'cuts'))  362 us
    all_gather x1, blocking collectives, body(): whole = lax.all_gather(resid, 'cuts', axis=0, tiled=True)  189 us
    all_gather x1, blocking collectives, body(): every = lax.all_gather(lines, 'cuts', axis=0)  187 us
  transfers between devices with their start and end apart: 1, of which 1 were waited for; matrix products, arithmetic and copies ran while one was open for 0% of the time, Pallas kernels for 0%

commit v1 on v0

--- a/solution.py
+++ b/solution.py
@@ -73,7 +73,9 @@
     pred = lax.psum_scatter(part, "cuts", scatter_dimension=0, tiled=True)
     kd = kdata[..., 0].transpose(3, 0, 2, 1).reshape(1, -1)
     resid = (pred.astype(F32) - kd.astype(F32)).astype(BF)
-    whole = lax.all_gather(resid, "cuts", axis=0, tiled=True)
+    whole = jnp.concatenate(
+        lax.all_to_all(jnp.stack([resid] * lax.axis_size("cuts")), "cuts", 0, 0), axis=0
+    )
     whole = whole.reshape(n_cuts, coils, 2, lpd, frames).transpose(3, 2, 1, 4, 0).astype(F32)
     spread = 0.0
     for sample in range(lpd):

time: 1550 us -> 1390 us (0.90)
  blocking collectives: 765 us -> 579 us
    all_gather x1 -> x0, blocking collectives: 189 us -> none  [body(): whole = lax.all_gather(resid, 'cuts', axis=0, tiled=True)]
  transfers between devices with their start and end apart: 1 -> 2, of which waited for: 1 -> 2; matrix products, arithmetic and copies ran while one was open for 0% -> 0% of each run, Pallas kernels for 0% -> 0%
where the time goes in v1:
time: 1390 us
  waiting for transfers between devices  695 us (50%)
  blocking collectives  579 us (42%)
  other arithmetic  49.8 us (4%)
  local copies, waits for them, and re-layouts  37.5 us (3%)
  between operations  15.6 us (1%)
    unnamed x2, waiting for transfers between devices  684 us
    psum x1, blocking collectives, body(): return (grad, lax.psum(shared, 'cuts'))  364 us
    all_gather x1, blocking collectives, body(): every = lax.all_gather(lines, 'cuts', axis=0)  187 us
  transfers between devices with their start and end apart: 2, of which 2 were waited for; matrix products, arithmetic and copies ran while one was open for 0% of the time, Pallas kernels for 0%

profile of v1, /device:TPU:0, one launch (start us, length us, event | category | flops | bytes accessed | tf_op | source)
XLA Modules:
  0.0 1388.5 jit_solution(18115466190048480171)
XLA Ops:
  7.2 0.7 copy.101
  7.9 9.1 all_gather.9
  17.0 0.1 copy.102
  17.1 0.8 convert_element_type.94
  17.9 186.8 %all-gather.1 = s32[64,64,2]{1,2,0:T(2,128)S(1)} all-gather(s32[1,64,2]{1,2,0:T(2,128)} %bitcast.242), channel_id=2, replica_groups=mesh['cuts'=64,'frame'=4] {'cuts'}, dimensions={0}, use_global_device_ids=true | all-gather | bytes 33280 | tf_op jit(solution)/shard_map/all_gather | solution.py:37
  205.0 0.9 convert_element_type.95
  206.0 0.6 fusion.25
  206.7 1.6 subtract_convert_fusion
  208.3 1.8 pad_maximum_fusion.2
  210.1 0.2 copy.146
  210.3 0.6 convolution_convert_fusion
  210.9 1.1 reshape.328
  212.0 0.6 fusion.33
  212.6 1.7 convolution_bitcast_fusion
  214.3 4.5 reshape.329
  218.9 12.0 fusion.43
  231.0 0.8 select_add_fusion.1
  231.8 0.3 subtract_reduce_fusion.2
  232.1 0.1 maximum_bitcast_fusion.1
  232.2 0.3 subtract_reduce_fusion.1
  232.5 0.1 maximum_bitcast_fusion.2
  232.5 0.2 maximum_bitcast_fusion
  232.8 0.8 copy.115
  233.6 1.3 convert_element_type.104
  234.9 0.1 reshape.330
  235.0 0.6 dynamic-slice
  235.6 683.9 %all-reduce.4.cloned.1.call-done = bf16[64,3072]{1,0:T(8,128)(2,1)} async-done(((bf16[64,3072]{1,0:T(8,128)(2,1)}), bf16[64,3072]{1,0:T(8,128)(2,1)}) %all-reduce.4.cloned.1.call-update) | async-done | bytes 393232
  919.6 1.5 fusion.40
  921.1 0.4 stack.93
  921.5 0.6 broadcast.617
  922.1 3.0 reduce.4
  925.1 1.0 reshape.354
  926.1 5.9 all-to-all-start
  932.1 0.6 dynamic-slice.2
  933.3 11.3 all-to-all-done
  944.6 0.3 reshape.355
  945.0 2.2 convert_reduce_fusion
  947.2 1.1 reshape.331
  948.3 1.2 fusion.44
  949.5 0.3 copy.120
  949.9 0.3 copy.121
  950.2 0.3 copy.118
  950.5 0.3 copy.117
  950.9 0.2 multiply_add_fusion.1
  951.1 0.2 copy-done.2
  951.4 0.2 multiply_add_fusion
  951.6 0.2 copy-done.29
  951.8 3.5 broadcast_select_fusion.3
  955.4 3.6 broadcast_select_fusion.7
  959.0 12.3 broadcast_select_fusion.2
  971.3 15.0 %fusion = bf16[12,2,2,64,4,64]{5,4,3,1,0,2:T(4,128)(2,1)S(1)} fusion(f32[12,2,2,64,1,64]{5,4,3,1,0,2:T(1,128)S(1)} %get-tuple-element.68, f32[12,2,2,64,1,64]{5,4,3,1,0,2:T(1,128)S(1)} %get-tuple-element.69, f32[12,2,2,64,1,64]{5,4,3,1,0,2:T(1,128)S(1)} %get-tuple-element.70, f32[12,2,2,64,1,64]{5,4,3,1,0,2:T(1,128)S(1)} %get-tuple-element.18, ...), kind=kLoop, calls=%fused_computation.1 | loop fusion | flops 6291456 | bytes 7864320 | tf_op jit(solution)/shard_map/convert_element_type | solution.py:88
  986.3 3.0 reshape.345
  989.3 2.9 convert_element_type.116
  992.2 2.6 fusion.11
  994.9 0.4 fusion.8
  995.3 0.8 copy.124
  996.1 0.5 reshape.343
  996.6 0.1 copy.129
  996.8 18.6 %all-reduce.1 = f32[2,32,64]{1,0,2:T(2,128)S(1)} all-reduce(f32[2,32,64]{1,0,2:T(2,128)S(1)} %copy.129), channel_id=4, replica_groups=mesh['cuts'=64,'frame'=4] {'frame'}, use_global_device_ids=true, to_apply=%region_7.8.clone | all-reduce | flops 4096 | bytes 32768
  1015.4 364.0 %psum.7 = f32[2,32,16]{1,0,2:T(2,128)S(1)} all-reduce(f32[2,32,16]{1,0,2:T(2,128)S(1)} %constant_dynamic-slice_fusion), channel_id=1, replica_groups=mesh['cuts'=64,'frame'=4] {'cuts'}, use_global_device_ids=true, to_apply=%region_8.9 | all-reduce | flops 1024 | bytes 8192 | tf_op jit(solution)/shard_map/psum | solution.py:100
  1379.4 0.6 copy.131
  1380.0 0.6 fusion.15
  1380.7 0.2 add_reduce_fusion
  1380.9 0.8 copy.130
  (88 shorter events, 0.6 us)
Async XLA Ops:
  7.2 912.4 %all-reduce.4.cloned.1.call-start = ((), (), s32[]{:S(2)}) async-start(), calls=%async_computation.1 | async-start | bytes 786432
  17.9 190.4 %copy-start.10 = (f32[12,2,256]{2,1,0:T(2,128)}, f32[12,2,256]{2,1,0:T(2,128)S(1)}, u32[]{:S(2)}) copy-start(f32[12,2,256]{2,1,0:T(2,128)S(1)} %get-tuple-element.60) | copy-start | bytes 73732
  17.9 190.4 %copy-start.12 = (f32[12,2,256]{2,1,0:T(2,128)}, f32[12,2,256]{2,1,0:T(2,128)S(1)}, u32[]{:S(2)}) copy-start(f32[12,2,256]{2,1,0:T(2,128)S(1)} %get-tuple-element.61) | copy-start | bytes 73732
  205.0 25.9 %copy-start.14 = (pred[64,64]{1,0:T(8,128)(4,1)}, pred[64,64]{1,0:T(8,128)(4,1)S(1)}, u32[]{:S(2)}) copy-start(pred[64,64]{1,0:T(8,128)(4,1)S(1)} %get-tuple-element.50) | copy-start | bytes 12292
  205.0 25.9 %copy-start.16 = (pred[64,64]{1,0:T(8,128)(4,1)}, pred[64,64]{1,0:T(8,128)(4,1)S(1)}, u32[]{:S(2)}) copy-start(pred[64,64]{1,0:T(8,128)(4,1)S(1)} %get-tuple-element.51) | copy-start | bytes 12292
  205.0 25.9 %copy-start.18 = (pred[64,64]{1,0:T(8,128)(4,1)}, pred[64,64]{1,0:T(8,128)(4,1)S(1)}, u32[]{:S(2)}) copy-start(pred[64,64]{1,0:T(8,128)(4,1)S(1)} %get-tuple-element.52) | copy-start | bytes 12292
  205.0 25.9 %copy-start.20 = (pred[64,64]{1,0:T(8,128)(4,1)}, pred[64,64]{1,0:T(8,128)(4,1)S(1)}, u32[]{:S(2)}) copy-start(pred[64,64]{1,0:T(8,128)(4,1)S(1)} %get-tuple-element.53) | copy-start | bytes 12292
  205.0 25.9 %copy-start.22 = (pred[64,64]{1,0:T(8,128)(4,1)}, pred[64,64]{1,0:T(8,128)(4,1)S(1)}, u32[]{:S(2)}) copy-start(pred[64,64]{1,0:T(8,128)(4,1)S(1)} %get-tuple-element.54) | copy-start | bytes 12292
  205.0 25.9 %copy-start.24 = (pred[64,64]{1,0:T(8,128)(4,1)}, pred[64,64]{1,0:T(8,128)(4,1)S(1)}, u32[]{:S(2)}) copy-start(pred[64,64]{1,0:T(8,128)(4,1)S(1)} %get-tuple-element.55) | copy-start | bytes 12292
  205.0 25.9 %copy-start.26 = (pred[64,64]{1,0:T(8,128)(4,1)}, pred[64,64]{1,0:T(8,128)(4,1)S(1)}, u32[]{:S(2)}) copy-start(pred[64,64]{1,0:T(8,128)(4,1)S(1)} %get-tuple-element.57) | copy-start | bytes 12292
  205.0 25.9 %copy-start.28 = (pred[64,64]{1,0:T(8,128)(4,1)}, pred[64,64]{1,0:T(8,128)(4,1)S(1)}, u32[]{:S(2)}) copy-start(pred[64,64]{1,0:T(8,128)(4,1)S(1)} %get-tuple-element.56) | copy-start | bytes 12292
  206.6 25.2 %copy-start.5 = (f32[2,64,64]{2,1,0:T(8,128)}, f32[2,64,64]{2,1,0:T(8,128)S(1)}, u32[]{:S(2)}) copy-start(f32[2,64,64]{2,1,0:T(8,128)S(1)} %get-tuple-element.42) | copy-start | bytes 98308
  206.6 25.5 %copy-start.1 = (f32[2,64,64]{2,1,0:T(8,128)}, f32[2,64,64]{2,1,0:T(8,128)S(1)}, u32[]{:S(2)}) copy-start(f32[2,64,64]{2,1,0:T(8,128)S(1)} %get-tuple-element.43) | copy-start | bytes 98308
  206.6 25.1 %copy-start.7 = (f32[2,64,64]{2,1,0:T(8,128)}, f32[2,64,64]{2,1,0:T(8,128)S(1)}, u32[]{:S(2)}) copy-start(f32[2,64,64]{2,1,0:T(8,128)S(1)} %get-tuple-element.45) | copy-start | bytes 98308
  206.7 25.5 %copy-start.3 = (f32[2,64,64]{2,1,0:T(8,128)}, f32[2,64,64]{2,1,0:T(8,128)S(1)}, u32[]{:S(2)}) copy-start(f32[2,64,64]{2,1,0:T(8,128)S(1)} %get-tuple-element.44) | copy-start | bytes 98308
  208.3 2.0 copy-start.32
  232.7 2.1 copy-start.31
  232.7 2.3 copy-start.34
  921.5 10.6 copy-start.33
  926.1 18.5 %all-to-all-start = ((bf16[64,2,1536]{2,1,0:T(2,128)(2,1)}), bf16[64,2,1536]{2,1,0:T(2,128)(2,1)S(1)}, u32[]{:S(2)}, u32[]{:S(2)}) async-start(bf16[64,2,1536]{2,1,0:T(2,128)(2,1)} %reshape.354), calls=%async_computation | async-start | bytes 786432 | tf_op jit(solution)/shard_map/all_to_all | solution.py:77
  949.5 1.3 copy-start.6
  949.5 1.3 copy-start.8
  950.5 0.8 copy-start.2
  950.5 0.9 copy-start.4
  951.1 0.7 copy-start.29
  951.8 3.5 copy-start.27
  955.4 3.6 copy-start.15
  955.4 3.6 copy-start.17
  955.4 3.6 copy-start.19
  955.4 3.6 copy-start.21
  955.4 3.6 copy-start.23
  955.4 3.6 copy-start.25
  992.2 2.6 copy-start
  992.2 2.6 copy-start.30
  995.3 384.8 %copy-start.9 = (bf16[2,256,512,1,1]{2,1,0,4,3:T(8,128)(2,1)S(1)}, bf16[2,256,512,1,1]{2,1,0,4,3:T(8,128)(2,1)}, u32[]{:S(2)}) copy-start(bf16[2,256,512,1,1]{2,1,0,4,3:T(8,128)(2,1)} %constant.75) | copy-start | bytes 1572868
  996.7 383.9 %copy-start.11 = (f32[12,2,256]{2,1,0:T(2,128)S(1)}, f32[12,2,256]{2,1,0:T(2,128)}, u32[]{:S(2)}) copy-start(f32[12,2,256]{2,1,0:T(2,128)} %copy-done.10) | copy-start | bytes 73732
  996.7 383.9 %copy-start.13 = (f32[12,2,256]{2,1,0:T(2,128)S(1)}, f32[12,2,256]{2,1,0:T(2,128)}, u32[]{:S(2)}) copy-start(f32[12,2,256]{2,1,0:T(2,128)} %copy-done.12) | copy-start | bytes 73732
Sparse Core Ops, SparseCore 0:
  235.0 684.5 all-reduce.3
